TPU v7x, 32 devices: a whole 2x2x4 slice. The times are simulated.
32 devices in a mesh: dp: 4 (over y, x), feat: 8 (over z, core).
Axes of the slice: x: 2, y: 2, z: 4, core: 2. Of those that a mesh axis runs over, the one named last changes fastest.
Arguments:
- features: bfloat16 [8192, 1024], P('dp', 'feat'), may hold values from -6 to 6
- owners: int32 [8, 64, 1], P('feat', 'dp'), may hold values from 0 to 3; in each aligned block of 16 rows (0 to 15, 16 to 31, ..., all dimensions but the last counted through in order) at most 8 rows name the same one
- weights: bfloat16 [8, 4096], P(None, ('dp', 'feat')), may hold values from -0.1875 to 0.1875
- labels: int32 [8192], P('dp'), may hold values from 0 to 7
Outputs:
- hessian: float32 [32, 1024, 1024], P(('dp', 'feat'))
- gradient: float32 [8, 4096], P(None, ('dp', 'feat'))
Inputs may be any that keep to these rules, and one draw needn't show every extreme that they name: `owners`: among the 16 row blocks of one index of dp, in one tile column, at most 8 name the same owner, a bound that some block reaches.
All inputs are finite; a program needn't handle non-finite values.
Results may differ from a plain program's by a relative error of at most 0.0023.
Values may be sent and summed in bfloat16 or wider, within the bound.
A program may use at most 64 MiB of HBM per device.

v0:
```python
import math
import jax
import jax.numpy as jnp
from jax import lax
from jax.sharding import PartitionSpec as P


def normalize(logits):
    expo = jnp.exp(logits)
    return expo / jnp.sum(expo, axis=-1, keepdims=True)


def spread_diagonal(diag_part, classes, width):
    blocks = diag_part.reshape(classes, width, width)
    unit = jnp.eye(classes, dtype=jnp.float32)
    return (unit[:, None, :, None] * blocks[:, :, None, :]).reshape(
        classes * width, classes * width
    )


def arrange(target, groups, capacity):
    count = target.shape[0]
    order = jnp.arange(count, dtype=jnp.int32)
    earlier = (order[None, :] < order[:, None]) & (target[None, :] == target[:, None])
    ranking = jnp.sum(earlier.astype(jnp.int32), axis=1)
    slot_index = jnp.arange(groups * capacity, dtype=jnp.int32)
    slot_group = slot_index // capacity
    slot_rank = slot_index % capacity
    hits = (target[None, :] == slot_group[:, None]) & (ranking[None, :] == slot_rank[:, None])
    source = jnp.sum(jnp.where(hits, order[None, :], 0), axis=1)
    filled = jnp.any(hits, axis=1)
    return (source, filled)


def select_blocks(block_data, source, filled):
    picked = jnp.take(block_data, source, axis=0)
    return jnp.where(filled[:, None, None], picked, jnp.zeros_like(picked))


def accumulate(totals, feature_rows, prob_rows, classes):
    count, width = feature_rows.shape
    group = math.gcd(count, 512)

    def turn(step, state):
        hess_acc, grad_acc = state
        begin = step * group
        x_part = lax.dynamic_slice_in_dim(feature_rows, begin, group, 0)
        p_part = lax.dynamic_slice_in_dim(prob_rows, begin, group, 0)
        probs = p_part[:, :classes].astype(jnp.float32)
        resid = p_part[:, classes:]
        kron_rows = (
            (probs[:, :, None] * x_part.astype(jnp.float32)[:, None, :])
            .reshape(group, classes * width)
            .astype(jnp.bfloat16)
        )
        joint = jnp.concatenate([kron_rows, x_part], axis=1)
        product = lax.dot_general(
            kron_rows, joint, (((0,), (0,)), ((), ())), preferred_element_type=jnp.float32
        )
        square = product[:, : classes * width]
        diag_part = product[:, classes * width :]
        grad_term = lax.dot_general(
            resid, x_part, (((0,), (0,)), ((), ())), preferred_element_type=jnp.float32
        )
        return (
            hess_acc + spread_diagonal(diag_part, classes, width) - square,
            grad_acc + grad_term,
        )

    return lax.fori_loop(0, count // group, turn, totals)


def per_device(features, owners, weights, labels):
    rows, width = features.shape
    classes = weights.shape[0]
    blocks = owners.shape[1]
    block_rows = rows // blocks
    dp_count = lax.axis_size("dp")
    capacity = max(2, 2 * ((blocks + dp_count - 1) // dp_count))
    target = owners.reshape(blocks)
    gathered = lax.all_gather(weights, "dp", axis=1, tiled=True)
    table = gathered.reshape(classes, dp_count, width)
    every_owner = jnp.einsum("rt,cut->ruc", features, table, preferred_element_type=jnp.float32)
    row_owner = jnp.repeat(target, block_rows)
    owner_mask = (row_owner[:, None] == jnp.arange(dp_count, dtype=jnp.int32)[None, :]).astype(
        jnp.float32
    )
    partial_logits = jnp.sum(every_owner * owner_mask[:, :, None], axis=1)
    logits = lax.psum(partial_logits, "feat")
    probs = normalize(logits)
    onehot = (labels[:, None] == jnp.arange(classes, dtype=jnp.int32)[None, :]).astype(jnp.float32)
    probs_half = probs.astype(jnp.bfloat16)
    resid = (probs - onehot).astype(jnp.bfloat16)
    paired = jnp.concatenate([probs_half, resid], axis=1)
    feature_blocks = features.reshape(blocks, block_rows, width)
    paired_blocks = paired.reshape(blocks, block_rows, 2 * classes)
    start = (
        jnp.zeros((classes * width, classes * width), jnp.float32),
        jnp.zeros((classes, width), jnp.float32),
    )
    source, filled = arrange(target, dp_count, capacity)
    sent_features = select_blocks(feature_blocks, source, filled)
    sent_paired = select_blocks(paired_blocks, source, filled)
    got_features, got_paired = (
        lax.all_to_all(sent_features, "dp", split_axis=0, concat_axis=0, tiled=True),
        lax.all_to_all(sent_paired, "dp", split_axis=0, concat_axis=0, tiled=True),
    )
    hess_acc, grad_acc = accumulate(
        start, got_features.reshape(-1, width), got_paired.reshape(-1, 2 * classes), classes
    )
    hessian = (hess_acc / block_rows)[None]
    gradient = grad_acc / block_rows
    return (hessian, gradient)


def solution(mesh):
    in_specs = (P("dp", "feat"), P("feat", "dp", None), P(None, ("dp", "feat")), P("dp"))
    out_specs = (P(("dp", "feat"), None, None), P(None, ("dp", "feat")))
    return jax.shard_map(
        per_device, mesh=mesh, in_specs=in_specs, out_specs=out_specs, check_vma=False
    )
```

profile of v0, /device:TPU:0, one launch (start us, length us, event | category | flops | bytes accessed | tf_op | source)
XLA Modules:
  0.0 189.6 jit_solution(15932147110795025760)
XLA Ops:
  7.2 0.8 broadcast_bitcast_fusion
  8.0 9.6 %all_gather.3 = bf16[8,512]{1,0:T(8,128)(2,1)S(1)} all-gather(bf16[8,128]{1,0:T(8,128)(2,1)} %param.8), channel_id=1, replica_groups=mesh['dp'=4,'feat'=8] {'dp'}, dimensions={1}, use_global_device_ids=true | all-gather | bytes 10240 | tf_op jit(solution)/shard_map/all_gather | solution.py:81
  17.7 0.9 fusion.9
  18.6 0.9 convert_reduce_fusion
  21.0 0.7 gather_fusion.1
  21.8 50.8 %all-reduce.2.cloned.1.call-done = f32[2048,8]{0,1:T(8,128)} async-done(((f32[2048,8]{0,1:T(8,128)}), f32[2048,8]{0,1:T(8,128)}) %all-reduce.2.cloned.1.call-update) | async-done | bytes 65552 | tf_op jit(solution)/shard_map/psum | solution.py:89
  72.6 0.9 exponential_reduce_fusion
  73.5 0.9 fusion.12
  75.0 0.8 select_select_fusion.1
  75.8 3.6 %all-to-all-start = ((bf16[32,128,16]{1,2,0:T(8,128)(2,1)}), bf16[32,128,16]{1,2,0:T(8,128)(2,1)S(1)}, u32[]{:S(2)}, u32[]{:S(2)}) async-start(bf16[32,128,16]{1,2,0:T(8,128)(2,1)} %select_select_fusion.1), calls=%async_computation | async-start | bytes 262144 | tf_op jit(solution)/shard_map/all_to_all | solution.py:106
  79.4 1.2 select_select_fusion
  80.6 3.8 %all-to-all-done = bf16[32,128,16]{1,2,0:T(8,128)(2,1)S(1)} async-done(((bf16[32,128,16]{1,2,0:T(8,128)(2,1)}), bf16[32,128,16]{1,2,0:T(8,128)(2,1)S(1)}, u32[]{:S(2)}, u32[]{:S(2)}) %all-to-all-start) | async-done | bytes 131104 | tf_op jit(solution)/shard_map/all_to_all | solution.py:106
  84.4 3.5 %all-to-all-start.1 = ((bf16[32,128,128]{2,1,0:T(8,128)(2,1)}), bf16[32,128,128]{2,1,0:T(8,128)(2,1)S(1)}, u32[]{:S(2)}, u32[]{:S(2)}) async-start(bf16[32,128,128]{2,1,0:T(8,128)(2,1)} %select_select_fusion), calls=%async_computation.1 | async-start | bytes 2097152 | tf_op jit(solution)/shard_map/all_to_all | solution.py:105
  88.0 10.9 %all-to-all-done.1 = bf16[32,128,128]{2,1,0:T(8,128)(2,1)S(1)} async-done(((bf16[32,128,128]{2,1,0:T(8,128)(2,1)}), bf16[32,128,128]{2,1,0:T(8,128)(2,1)S(1)}, u32[]{:S(2)}, u32[]{:S(2)}) %all-to-all-start.1) | async-done | bytes 1048608 | tf_op jit(solution)/shard_map/all_to_all | solution.py:105
  98.9 78.2 %while.16 = (s32[]{:T(128)}, f32[1024,1024]{1,0:T(8,128)}, f32[8,128]{1,0:T(8,128)S(1)}, bf16[4096,16]{0,1:T(8,128)(2,1)S(1)}, bf16[4096,128]{1,0:T(8,128)(2,1)S...) while((s32[]{:T(128)}, f32[1024,1024]{1,0:T(8,128)}, f32[8,128]{1,0:T(8,128)S(1)}, ...), condition=%wide.region_7.8_spmd.clone, body=%wide.region_6.7_spmd.clone.sunk | while | flops 1216682112 | bytes 66151160 | solution.py:70
  100.2 1.6 fusion.34
  102.2 1.8 copy-done.1
  103.9 2.7 %fusion.36 = f32[1024,1024]{1,0:T(8,128)S(1)} fusion(f32[128,8,8,128]{3,2,1,0:T(8,128)S(1)} %bitcast.61, f32[1024,1152]{1,0:T(8,128)S(1)} %fusion.34, f32[1024,1024]{1,0:T(8,128)S(1)} %copy-done.1, pred[]{:T(512)S(6)} %compare.8), kind=kLoop, calls=%fused_computation.3.clone.1 | loop fusion | flops 3145728 | bytes 16777216 | tf_op jit(solution)/shard_map/while/body/eval_jaxpr/sub | solution.py:66
  106.6 2.0 %copy-done.2 = f32[1024,1024]{1,0:T(8,128)} copy-done((f32[1024,1024]{1,0:T(8,128)}, f32[1024,1024]{1,0:T(8,128)S(1)}, u32[]{:S(2)}) %copy-start.2) | copy-done | bytes 4194328 | tf_op jit(solution)/shard_map/while
  109.9 1.6 fusion.34
  111.9 1.8 copy-done.1
  113.7 2.7 %fusion.36 = f32[1024,1024]{1,0:T(8,128)S(1)} fusion(f32[128,8,8,128]{3,2,1,0:T(8,128)S(1)} %bitcast.61, f32[1024,1152]{1,0:T(8,128)S(1)} %fusion.34, f32[1024,1024]{1,0:T(8,128)S(1)} %copy-done.1, pred[]{:T(512)S(6)} %compare.8), kind=kLoop, calls=%fused_computation.3.clone.1 | loop fusion | flops 3145728 | bytes 16777216 | tf_op jit(solution)/shard_map/while/body/eval_jaxpr/sub | solution.py:66
  116.4 2.0 %copy-done.2 = f32[1024,1024]{1,0:T(8,128)} copy-done((f32[1024,1024]{1,0:T(8,128)}, f32[1024,1024]{1,0:T(8,128)S(1)}, u32[]{:S(2)}) %copy-start.2) | copy-done | bytes 4194328 | tf_op jit(solution)/shard_map/while
  119.7 1.6 fusion.34
  121.7 1.8 copy-done.1
  123.5 2.7 %fusion.36 = f32[1024,1024]{1,0:T(8,128)S(1)} fusion(f32[128,8,8,128]{3,2,1,0:T(8,128)S(1)} %bitcast.61, f32[1024,1152]{1,0:T(8,128)S(1)} %fusion.34, f32[1024,1024]{1,0:T(8,128)S(1)} %copy-done.1, pred[]{:T(512)S(6)} %compare.8), kind=kLoop, calls=%fused_computation.3.clone.1 | loop fusion | flops 3145728 | bytes 16777216 | tf_op jit(solution)/shard_map/while/body/eval_jaxpr/sub | solution.py:66
  126.2 2.0 %copy-done.2 = f32[1024,1024]{1,0:T(8,128)} copy-done((f32[1024,1024]{1,0:T(8,128)}, f32[1024,1024]{1,0:T(8,128)S(1)}, u32[]{:S(2)}) %copy-start.2) | copy-done | bytes 4194328 | tf_op jit(solution)/shard_map/while
  129.5 1.6 fusion.34
  131.5 1.8 copy-done.1
  133.3 2.7 %fusion.36 = f32[1024,1024]{1,0:T(8,128)S(1)} fusion(f32[128,8,8,128]{3,2,1,0:T(8,128)S(1)} %bitcast.61, f32[1024,1152]{1,0:T(8,128)S(1)} %fusion.34, f32[1024,1024]{1,0:T(8,128)S(1)} %copy-done.1, pred[]{:T(512)S(6)} %compare.8), kind=kLoop, calls=%fused_computation.3.clone.1 | loop fusion | flops 3145728 | bytes 16777216 | tf_op jit(solution)/shard_map/while/body/eval_jaxpr/sub | solution.py:66
  136.0 2.0 %copy-done.2 = f32[1024,1024]{1,0:T(8,128)} copy-done((f32[1024,1024]{1,0:T(8,128)}, f32[1024,1024]{1,0:T(8,128)S(1)}, u32[]{:S(2)}) %copy-start.2) | copy-done | bytes 4194328 | tf_op jit(solution)/shard_map/while
  139.3 1.6 fusion.34
  141.3 1.8 copy-done.1
  143.1 2.7 %fusion.36 = f32[1024,1024]{1,0:T(8,128)S(1)} fusion(f32[128,8,8,128]{3,2,1,0:T(8,128)S(1)} %bitcast.61, f32[1024,1152]{1,0:T(8,128)S(1)} %fusion.34, f32[1024,1024]{1,0:T(8,128)S(1)} %copy-done.1, pred[]{:T(512)S(6)} %compare.8), kind=kLoop, calls=%fused_computation.3.clone.1 | loop fusion | flops 3145728 | bytes 16777216 | tf_op jit(solution)/shard_map/while/body/eval_jaxpr/sub | solution.py:66
  145.8 2.0 %copy-done.2 = f32[1024,1024]{1,0:T(8,128)} copy-done((f32[1024,1024]{1,0:T(8,128)}, f32[1024,1024]{1,0:T(8,128)S(1)}, u32[]{:S(2)}) %copy-start.2) | copy-done | bytes 4194328 | tf_op jit(solution)/shard_map/while
  149.1 1.6 fusion.34
  151.1 1.8 copy-done.1
  152.8 2.7 %fusion.36 = f32[1024,1024]{1,0:T(8,128)S(1)} fusion(f32[128,8,8,128]{3,2,1,0:T(8,128)S(1)} %bitcast.61, f32[1024,1152]{1,0:T(8,128)S(1)} %fusion.34, f32[1024,1024]{1,0:T(8,128)S(1)} %copy-done.1, pred[]{:T(512)S(6)} %compare.8), kind=kLoop, calls=%fused_computation.3.clone.1 | loop fusion | flops 3145728 | bytes 16777216 | tf_op jit(solution)/shard_map/while/body/eval_jaxpr/sub | solution.py:66
  155.5 2.0 %copy-done.2 = f32[1024,1024]{1,0:T(8,128)} copy-done((f32[1024,1024]{1,0:T(8,128)}, f32[1024,1024]{1,0:T(8,128)S(1)}, u32[]{:S(2)}) %copy-start.2) | copy-done | bytes 4194328 | tf_op jit(solution)/shard_map/while
  158.8 1.6 fusion.34
  160.9 1.8 copy-done.1
  162.6 2.7 %fusion.36 = f32[1024,1024]{1,0:T(8,128)S(1)} fusion(f32[128,8,8,128]{3,2,1,0:T(8,128)S(1)} %bitcast.61, f32[1024,1152]{1,0:T(8,128)S(1)} %fusion.34, f32[1024,1024]{1,0:T(8,128)S(1)} %copy-done.1, pred[]{:T(512)S(6)} %compare.8), kind=kLoop, calls=%fused_computation.3.clone.1 | loop fusion | flops 3145728 | bytes 16777216 | tf_op jit(solution)/shard_map/while/body/eval_jaxpr/sub | solution.py:66
  165.3 2.0 %copy-done.2 = f32[1024,1024]{1,0:T(8,128)} copy-done((f32[1024,1024]{1,0:T(8,128)}, f32[1024,1024]{1,0:T(8,128)S(1)}, u32[]{:S(2)}) %copy-start.2) | copy-done | bytes 4194328 | tf_op jit(solution)/shard_map/while
  168.6 1.6 fusion.34
  170.6 1.8 copy-done.1
  172.4 2.7 %fusion.36 = f32[1024,1024]{1,0:T(8,128)S(1)} fusion(f32[128,8,8,128]{3,2,1,0:T(8,128)S(1)} %bitcast.61, f32[1024,1152]{1,0:T(8,128)S(1)} %fusion.34, f32[1024,1024]{1,0:T(8,128)S(1)} %copy-done.1, pred[]{:T(512)S(6)} %compare.8), kind=kLoop, calls=%fused_computation.3.clone.1 | loop fusion | flops 3145728 | bytes 16777216 | tf_op jit(solution)/shard_map/while/body/eval_jaxpr/sub | solution.py:66
  175.1 2.0 %copy-done.2 = f32[1024,1024]{1,0:T(8,128)} copy-done((f32[1024,1024]{1,0:T(8,128)}, f32[1024,1024]{1,0:T(8,128)S(1)}, u32[]{:S(2)}) %copy-start.2) | copy-done | bytes 4194328 | tf_op jit(solution)/shard_map/while
  177.7 5.0 %multiply_bitcast_fusion = f32[1,1024,1024]{2,1,0:T(8,128)} fusion(f32[1024,1024]{1,0:T(8,128)} %get-tuple-element.97), kind=kLoop, calls=%fused_computation.18 | loop fusion | flops 1048576 | bytes 8388608 | tf_op jit(solution)/shard_map/broadcast_in_dim | solution.py:111
  (105 shorter events, 16.1 us)
Async XLA Ops:
  7.2 10.5 %copy-start = (bf16[2048,128]{1,0:T(8,128)(2,1)S(1)}, bf16[2048,128]{1,0:T(8,128)(2,1)}, u32[]{:S(2)}) copy-start(bf16[2048,128]{1,0:T(8,128)(2,1)} %param.6) | copy-start | bytes 1572868
  7.2 65.4 %all-reduce.2.cloned.1.call-start = ((), (), s32[]{:S(2)}) async-start(), calls=%async_computation.2 | async-start | bytes 131072 | tf_op jit(solution)/shard_map/psum | solution.py:89
  75.8 8.7 %all-to-all-start = ((bf16[32,128,16]{1,2,0:T(8,128)(2,1)}), bf16[32,128,16]{1,2,0:T(8,128)(2,1)S(1)}, u32[]{:S(2)}, u32[]{:S(2)}) async-start(bf16[32,128,16]{1,2,0:T(8,128)(2,1)} %select_select_fusion.1), calls=%async_computation | async-start | bytes 262144 | tf_op jit(solution)/shard_map/all_to_all | solution.py:106
  84.4 14.4 %all-to-all-start.1 = ((bf16[32,128,128]{2,1,0:T(8,128)(2,1)}), bf16[32,128,128]{2,1,0:T(8,128)(2,1)S(1)}, u32[]{:S(2)}, u32[]{:S(2)}) async-start(bf16[32,128,128]{2,1,0:T(8,128)(2,1)} %select_select_fusion), calls=%async_computation.1 | async-start | bytes 2097152 | tf_op jit(solution)/shard_map/all_to_all | solution.py:105
  101.7 2.2 %copy-start.1 = (f32[1024,1024]{1,0:T(8,128)S(1)}, f32[1024,1024]{1,0:T(8,128)}, u32[]{:S(2)}) copy-start(f32[1024,1024]{1,0:T(8,128)} %get-tuple-element.179) | copy-start | bytes 12582916 | tf_op jit(solution)/shard_map/while
  106.6 2.0 %copy-start.2 = (f32[1024,1024]{1,0:T(8,128)}, f32[1024,1024]{1,0:T(8,128)S(1)}, u32[]{:S(2)}) copy-start(f32[1024,1024]{1,0:T(8,128)S(1)} %fusion.36) | copy-start | bytes 12582916 | tf_op jit(solution)/shard_map/while
  111.5 2.2 %copy-start.1 = (f32[1024,1024]{1,0:T(8,128)S(1)}, f32[1024,1024]{1,0:T(8,128)}, u32[]{:S(2)}) copy-start(f32[1024,1024]{1,0:T(8,128)} %get-tuple-element.179) | copy-start | bytes 12582916 | tf_op jit(solution)/shard_map/while
  116.4 2.0 %copy-start.2 = (f32[1024,1024]{1,0:T(8,128)}, f32[1024,1024]{1,0:T(8,128)S(1)}, u32[]{:S(2)}) copy-start(f32[1024,1024]{1,0:T(8,128)S(1)} %fusion.36) | copy-start | bytes 12582916 | tf_op jit(solution)/shard_map/while
  121.3 2.2 %copy-start.1 = (f32[1024,1024]{1,0:T(8,128)S(1)}, f32[1024,1024]{1,0:T(8,128)}, u32[]{:S(2)}) copy-start(f32[1024,1024]{1,0:T(8,128)} %get-tuple-element.179) | copy-start | bytes 12582916 | tf_op jit(solution)/shard_map/while
  126.2 2.0 %copy-start.2 = (f32[1024,1024]{1,0:T(8,128)}, f32[1024,1024]{1,0:T(8,128)S(1)}, u32[]{:S(2)}) copy-start(f32[1024,1024]{1,0:T(8,128)S(1)} %fusion.36) | copy-start | bytes 12582916 | tf_op jit(solution)/shard_map/while
  131.1 2.2 %copy-start.1 = (f32[1024,1024]{1,0:T(8,128)S(1)}, f32[1024,1024]{1,0:T(8,128)}, u32[]{:S(2)}) copy-start(f32[1024,1024]{1,0:T(8,128)} %get-tuple-element.179) | copy-start | bytes 12582916 | tf_op jit(solution)/shard_map/while
  136.0 2.0 %copy-start.2 = (f32[1024,1024]{1,0:T(8,128)}, f32[1024,1024]{1,0:T(8,128)S(1)}, u32[]{:S(2)}) copy-start(f32[1024,1024]{1,0:T(8,128)S(1)} %fusion.36) | copy-start | bytes 12582916 | tf_op jit(solution)/shard_map/while
  140.9 2.2 %copy-start.1 = (f32[1024,1024]{1,0:T(8,128)S(1)}, f32[1024,1024]{1,0:T(8,128)}, u32[]{:S(2)}) copy-start(f32[1024,1024]{1,0:T(8,128)} %get-tuple-element.179) | copy-start | bytes 12582916 | tf_op jit(solution)/shard_map/while
  145.8 2.0 %copy-start.2 = (f32[1024,1024]{1,0:T(8,128)}, f32[1024,1024]{1,0:T(8,128)S(1)}, u32[]{:S(2)}) copy-start(f32[1024,1024]{1,0:T(8,128)S(1)} %fusion.36) | copy-start | bytes 12582916 | tf_op jit(solution)/shard_map/while
  150.6 2.2 %copy-start.1 = (f32[1024,1024]{1,0:T(8,128)S(1)}, f32[1024,1024]{1,0:T(8,128)}, u32[]{:S(2)}) copy-start(f32[1024,1024]{1,0:T(8,128)} %get-tuple-element.179) | copy-start | bytes 12582916 | tf_op jit(solution)/shard_map/while
  155.5 2.0 %copy-start.2 = (f32[1024,1024]{1,0:T(8,128)}, f32[1024,1024]{1,0:T(8,128)S(1)}, u32[]{:S(2)}) copy-start(f32[1024,1024]{1,0:T(8,128)S(1)} %fusion.36) | copy-start | bytes 12582916 | tf_op jit(solution)/shard_map/while
  160.4 2.2 %copy-start.1 = (f32[1024,1024]{1,0:T(8,128)S(1)}, f32[1024,1024]{1,0:T(8,128)}, u32[]{:S(2)}) copy-start(f32[1024,1024]{1,0:T(8,128)} %get-tuple-element.179) | copy-start | bytes 12582916 | tf_op jit(solution)/shard_map/while
  165.3 2.0 %copy-start.2 = (f32[1024,1024]{1,0:T(8,128)}, f32[1024,1024]{1,0:T(8,128)S(1)}, u32[]{:S(2)}) copy-start(f32[1024,1024]{1,0:T(8,128)S(1)} %fusion.36) | copy-start | bytes 12582916 | tf_op jit(solution)/shard_map/while
  170.2 2.2 %copy-start.1 = (f32[1024,1024]{1,0:T(8,128)S(1)}, f32[1024,1024]{1,0:T(8,128)}, u32[]{:S(2)}) copy-start(f32[1024,1024]{1,0:T(8,128)} %get-tuple-element.179) | copy-start | bytes 12582916 | tf_op jit(solution)/shard_map/while
  175.1 2.0 %copy-start.2 = (f32[1024,1024]{1,0:T(8,128)}, f32[1024,1024]{1,0:T(8,128)S(1)}, u32[]{:S(2)}) copy-start(f32[1024,1024]{1,0:T(8,128)S(1)} %fusion.36) | copy-start | bytes 12582916 | tf_op jit(solution)/shard_map/while
Sparse Core Ops, SparseCore 0:
  18.7 53.8 all-reduce.1
where the time goes:
time: 190 us
  waiting for transfers between devices  65.6 us (35%)
  other arithmetic  42.1 us (22%)
  local copies, waits for them, and re-layouts  35.8 us (19%)
  matrix products  14.6 us (8%)
  between operations  14.1 us (7%)
  blocking collectives  9.63 us (5%)
  starting transfers between devices  7.2 us (4%)
    psum x1, waiting for transfers between devices, per_device(): logits = lax.psum(partial_logits, 'feat')  50.8 us
    while x40, local copies, waits for them, and re-layouts  32.4 us
    sub x8, other arithmetic, turn(): hess_acc + spread_diagonal(diag_part, classes, width) - square  21.6 us
    dot_general x8, matrix products, turn(): lax.dot_general(kron_rows, joint, (((0,), (0,)), ((), ())), preferred_ele...  12.6 us
    all_to_all x1, waiting for transfers between devices, per_device(): lax.all_to_all(sent_features, 'dp', split_axis=0, concat_axis=0, tiled=True)  10.9 us
    all_gather x1, blocking collectives, per_device(): gathered = lax.all_gather(weights, 'dp', axis=1, tiled=True)  9.63 us
    convert_element_type x8, other arithmetic, turn(): kron_rows = (probs[:, :, None] * x_part.astype(jnp.float32)[:, None, :])....  5.53 us
    broadcast_in_dim x1, other arithmetic, per_device(): hessian = (hess_acc / block_rows)[None]  5.04 us
  transfers between devices with their start and end apart: 3, of which 3 were waited for; matrix products, arithmetic and copies ran while one was open for 2% of the time, Pallas kernels for 0%

commit v1 on v0

--- a/solution.py
+++ b/solution.py
@@ -3,6 +3,38 @@
 import jax.numpy as jnp
 from jax import lax
 from jax.sharding import PartitionSpec as P
+
+
+def group_sheet(buf, dimension_no, chunk):
+    item_now, block_last = (buf.shape[:dimension_no], buf.shape[dimension_no + 1 :])
+    low = buf.reshape(*item_now, chunk, -1, *block_last)
+    return jnp.moveaxis(low, dimension_no, 0)
+
+
+def _deliver_goods(view, array_dim):
+    view = jnp.moveaxis(view, 0, array_dim)
+    arr_next = view.shape
+    return view.reshape(
+        *arr_next[:array_dim],
+        arr_next[array_dim] * arr_next[array_dim + 1],
+        *arr_next[array_dim + 2 :]
+    )
+
+
+def masks_run(q_in, z_in, mine, mesh_ax="dp"):
+    inter = lax.axis_index(mesh_ax)
+    opened = lax.axis_size(mesh_ax)
+    wide_out, local_now = (opened, inter)
+    y2 = group_sheet(z_in, q_in, wide_out)
+    passed = y2
+    for to_i in range(1, wide_out):
+        piece_next, extra = ((local_now + to_i) % wide_out, (local_now - to_i) % wide_out)
+        p_next = lax.dynamic_index_in_dim(y2, piece_next, 0)
+        before = lax.ppermute(
+            p_next, axis_name=mesh_ax, perm=[(q, (q + to_i) % wide_out) for q in range(wide_out)]
+        )
+        passed = lax.dynamic_update_slice_in_dim(passed, before, extra, axis=0)
+    return _deliver_goods(passed, mine)
 
 
 def normalize(logits):
@@ -102,7 +134,7 @@
     sent_features = select_blocks(feature_blocks, source, filled)
     sent_paired = select_blocks(paired_blocks, source, filled)
     got_features, got_paired = (
-        lax.all_to_all(sent_features, "dp", split_axis=0, concat_axis=0, tiled=True),
+        masks_run(0, sent_features, 0),
         lax.all_to_all(sent_paired, "dp", split_axis=0, concat_axis=0, tiled=True),
     )
     hess_acc, grad_acc = accumulate(

time: 190 us -> 183 us (0.963); the launches traced: 190 us -> 180 us
  waiting for transfers between devices: 65.6 us -> 54.8 us
    all_to_all x1 -> x0, waiting for transfers between devices: 10.9 us -> none  [per_device(): lax.all_to_all(sent_features, 'dp', split_axis=0, concat_axis=0, tiled=True)]
    ppermute x0 -> x3, starting transfers between devices: none -> 4.96 us  [masks_run(): lax.ppermute(p_next, axis_name=mesh_ax, perm=[(q, (q + to_i) % wide_out)...]
    ppermute x0 -> x3, waiting for transfers between devices: none -> 4.05 us  [masks_run(): lax.ppermute(p_next, axis_name=mesh_ax, perm=[(q, (q + to_i) % wide_out)...]
    all_to_all x1 -> x0, starting transfers between devices: 3.52 us -> none  [per_device(): lax.all_to_all(sent_features, 'dp', split_axis=0, concat_axis=0, tiled=True)]
    all_to_all x1, waiting for transfers between devices: 3.82 us -> 1.75 us  [per_device(): lax.all_to_all(sent_paired, 'dp', split_axis=0, concat_axis=0, tiled=True)]
  transfers between devices with their start and end apart: 3 -> 5, of which waited for: 3 -> 3; matrix products, arithmetic and copies ran while one was open for 2% -> 4% of each run, Pallas kernels for 0% -> 0%
where the time goes in v1:
time: 183 us; the launch traced here: 180 us
  waiting for transfers between devices  54.8 us (30%)
  other arithmetic  41.1 us (22%)
  local copies, waits for them, and re-layouts  36.2 us (20%)
  matrix products  14.6 us (8%)
  between operations  14.2 us (8%)
  blocking collectives  9.63 us (5%)
  starting transfers between devices  8.65 us (5%)
    psum x1, waiting for transfers between devices, per_device(): logits = lax.psum(partial_logits, 'feat')  49 us
    while x40, local copies, waits for them, and re-layouts  32.4 us
    sub x8, other arithmetic, turn(): hess_acc + spread_diagonal(diag_part, classes, width) - square  21.6 us
    dot_general x8, matrix products, turn(): lax.dot_general(kron_rows, joint, (((0,), (0,)), ((), ())), preferred_ele...  12.6 us
    all_gather x1, blocking collectives, per_device(): gathered = lax.all_gather(weights, 'dp', axis=1, tiled=True)  9.63 us
    convert_element_type x8, other arithmetic, turn(): kron_rows = (probs[:, :, None] * x_part.astype(jnp.float32)[:, None, :])....  5.53 us
    broadcast_in_dim x1, other arithmetic, per_device(): hessian = (hess_acc / block_rows)[None]  5.04 us
    ppermute x3, starting transfers between devices, masks_run(): lax.ppermute(p_next, axis_name=mesh_ax, perm=[(q, (q + to_i) % wide_out)...  4.96 us
  transfers between devices with their start and end apart: 5, of which 3 were waited for; matrix products, arithmetic and copies ran while one was open for 4% of the time, Pallas kernels for 0%

profile of v1, /device:TPU:0, one launch (start us, length us, event | category | flops | bytes accessed | tf_op | source)
XLA Modules:
  0.0 179.8 jit_solution(5247616607592729983)
XLA Ops:
  7.2 0.8 broadcast_bitcast_fusion
  8.0 9.6 %all_gather.3 = bf16[8,512]{1,0:T(8,128)(2,1)S(1)} all-gather(bf16[8,128]{1,0:T(8,128)(2,1)} %param.8), channel_id=1, replica_groups=mesh['dp'=4,'feat'=8] {'dp'}, dimensions={1}, use_global_device_ids=true | all-gather | bytes 10240 | tf_op jit(solution)/shard_map/all_gather | solution.py:113
  17.7 0.9 fusion.9
  18.6 0.9 convert_reduce_fusion
  21.2 0.7 gather_fusion.1
  22.2 1.4 collective-permute-start
  23.7 49.0 %all-reduce.2.cloned.1.call-done = f32[2048,8]{0,1:T(8,128)} async-done(((f32[2048,8]{0,1:T(8,128)}), f32[2048,8]{0,1:T(8,128)}) %all-reduce.2.cloned.1.call-update) | async-done | bytes 65552 | tf_op jit(solution)/shard_map/psum | solution.py:121
  72.6 0.9 exponential_reduce_fusion
  73.5 0.9 fusion.12
  75.0 0.8 select_select_fusion.1
  75.8 3.6 %all-to-all-start = ((bf16[32,128,16]{1,2,0:T(8,128)(2,1)}), bf16[32,128,16]{1,2,0:T(8,128)(2,1)S(1)}, u32[]{:S(2)}, u32[]{:S(2)}) async-start(bf16[32,128,16]{1,2,0:T(8,128)(2,1)} %select_select_fusion.1), calls=%async_computation | async-start | bytes 262144 | tf_op jit(solution)/shard_map/all_to_all | solution.py:138
  79.6 3.0 %collective-permute-start.2 = (bf16[1,8,128,128]{3,2,1,0:T(8,128)(2,1)S(1)}, bf16[1,8,128,128]{3,2,1,0:T(8,128)(2,1)S(1)}, u32[]{:S(2)}, u32[]{:S(2)}) collective-permute-start(bf16[1,8,128,128]{3,2,1,0:T(8,128)(2,1)S(1)} %get-tuple-element.129), channel_id=1, source_target_pairs={{0,24},{8,0},{16,8},{24,16},{1,25},{9,1},{17,9},{25,17},{2,26},{10... | collective-permute-start | bytes 786440 | tf_op jit(solution)/shard_map/ppermute | solution.py:33
  83.1 1.7 all-to-all-done
  84.9 4.0 %collective-permute-done.1 = bf16[1,8,128,128]{3,2,1,0:T(8,128)(2,1)S(1)} collective-permute-done((bf16[1,8,128,128]{3,2,1,0:T(8,128)(2,1)S(1)}, bf16[1,8,128,128]{3,2,1,0:T(8,128)(2,1)S(1)}, u32[]{:S(2)}, u32[]{:S(2)}) %collective-permute-start.1) | collective-permute-done | bytes 262176 | tf_op jit(solution)/shard_map/ppermute | solution.py:33
  89.0 78.3 %while.16 = (s32[]{:T(128)}, f32[1024,1024]{1,0:T(8,128)}, f32[8,128]{1,0:T(8,128)S(1)}, bf16[4096,16]{0,1:T(8,128)(2,1)S(1)}, bf16[4096,128]{1,0:T(8,128)(2,1)S...) while((s32[]{:T(128)}, f32[1024,1024]{1,0:T(8,128)}, f32[8,128]{1,0:T(8,128)S(1)}, ...), condition=%wide.region_7.8_spmd.clone, body=%wide.region_6.7_spmd.clone.sunk | while | flops 1216682112 | bytes 66151160 | solution.py:102
  90.3 1.6 fusion.34
  92.3 1.8 copy-done.1
  94.1 2.7 %fusion.36 = f32[1024,1024]{1,0:T(8,128)S(1)} fusion(f32[128,8,8,128]{3,2,1,0:T(8,128)S(1)} %bitcast.62, f32[1024,1152]{1,0:T(8,128)S(1)} %fusion.34, f32[1024,1024]{1,0:T(8,128)S(1)} %copy-done.1, pred[]{:T(512)S(6)} %compare.14), kind=kLoop, calls=%fused_computation.3.clone.1 | loop fusion | flops 3145728 | bytes 16777216 | tf_op jit(solution)/shard_map/while/body/eval_jaxpr/sub | solution.py:98
  96.8 2.0 %copy-done.2 = f32[1024,1024]{1,0:T(8,128)} copy-done((f32[1024,1024]{1,0:T(8,128)}, f32[1024,1024]{1,0:T(8,128)S(1)}, u32[]{:S(2)}) %copy-start.2) | copy-done | bytes 4194328 | tf_op jit(solution)/shard_map/while
  100.1 1.6 fusion.34
  102.1 1.8 copy-done.1
  103.9 2.7 %fusion.36 = f32[1024,1024]{1,0:T(8,128)S(1)} fusion(f32[128,8,8,128]{3,2,1,0:T(8,128)S(1)} %bitcast.62, f32[1024,1152]{1,0:T(8,128)S(1)} %fusion.34, f32[1024,1024]{1,0:T(8,128)S(1)} %copy-done.1, pred[]{:T(512)S(6)} %compare.14), kind=kLoop, calls=%fused_computation.3.clone.1 | loop fusion | flops 3145728 | bytes 16777216 | tf_op jit(solution)/shard_map/while/body/eval_jaxpr/sub | solution.py:98
  106.6 2.0 %copy-done.2 = f32[1024,1024]{1,0:T(8,128)} copy-done((f32[1024,1024]{1,0:T(8,128)}, f32[1024,1024]{1,0:T(8,128)S(1)}, u32[]{:S(2)}) %copy-start.2) | copy-done | bytes 4194328 | tf_op jit(solution)/shard_map/while
  109.9 1.6 fusion.34
  111.9 1.8 copy-done.1
  113.7 2.7 %fusion.36 = f32[1024,1024]{1,0:T(8,128)S(1)} fusion(f32[128,8,8,128]{3,2,1,0:T(8,128)S(1)} %bitcast.62, f32[1024,1152]{1,0:T(8,128)S(1)} %fusion.34, f32[1024,1024]{1,0:T(8,128)S(1)} %copy-done.1, pred[]{:T(512)S(6)} %compare.14), kind=kLoop, calls=%fused_computation.3.clone.1 | loop fusion | flops 3145728 | bytes 16777216 | tf_op jit(solution)/shard_map/while/body/eval_jaxpr/sub | solution.py:98
  116.4 2.0 %copy-done.2 = f32[1024,1024]{1,0:T(8,128)} copy-done((f32[1024,1024]{1,0:T(8,128)}, f32[1024,1024]{1,0:T(8,128)S(1)}, u32[]{:S(2)}) %copy-start.2) | copy-done | bytes 4194328 | tf_op jit(solution)/shard_map/while
  119.7 1.6 fusion.34
  121.7 1.8 copy-done.1
  123.5 2.7 %fusion.36 = f32[1024,1024]{1,0:T(8,128)S(1)} fusion(f32[128,8,8,128]{3,2,1,0:T(8,128)S(1)} %bitcast.62, f32[1024,1152]{1,0:T(8,128)S(1)} %fusion.34, f32[1024,1024]{1,0:T(8,128)S(1)} %copy-done.1, pred[]{:T(512)S(6)} %compare.14), kind=kLoop, calls=%fused_computation.3.clone.1 | loop fusion | flops 3145728 | bytes 16777216 | tf_op jit(solution)/shard_map/while/body/eval_jaxpr/sub | solution.py:98
  126.2 2.0 %copy-done.2 = f32[1024,1024]{1,0:T(8,128)} copy-done((f32[1024,1024]{1,0:T(8,128)}, f32[1024,1024]{1,0:T(8,128)S(1)}, u32[]{:S(2)}) %copy-start.2) | copy-done | bytes 4194328 | tf_op jit(solution)/shard_map/while
  129.5 1.6 fusion.34
  131.5 1.8 copy-done.1
  133.2 2.7 %fusion.36 = f32[1024,1024]{1,0:T(8,128)S(1)} fusion(f32[128,8,8,128]{3,2,1,0:T(8,128)S(1)} %bitcast.62, f32[1024,1152]{1,0:T(8,128)S(1)} %fusion.34, f32[1024,1024]{1,0:T(8,128)S(1)} %copy-done.1, pred[]{:T(512)S(6)} %compare.14), kind=kLoop, calls=%fused_computation.3.clone.1 | loop fusion | flops 3145728 | bytes 16777216 | tf_op jit(solution)/shard_map/while/body/eval_jaxpr/sub | solution.py:98
  135.9 2.0 %copy-done.2 = f32[1024,1024]{1,0:T(8,128)} copy-done((f32[1024,1024]{1,0:T(8,128)}, f32[1024,1024]{1,0:T(8,128)S(1)}, u32[]{:S(2)}) %copy-start.2) | copy-done | bytes 4194328 | tf_op jit(solution)/shard_map/while
  139.2 1.6 fusion.34
  141.2 1.8 copy-done.1
  143.0 2.7 %fusion.36 = f32[1024,1024]{1,0:T(8,128)S(1)} fusion(f32[128,8,8,128]{3,2,1,0:T(8,128)S(1)} %bitcast.62, f32[1024,1152]{1,0:T(8,128)S(1)} %fusion.34, f32[1024,1024]{1,0:T(8,128)S(1)} %copy-done.1, pred[]{:T(512)S(6)} %compare.14), kind=kLoop, calls=%fused_computation.3.clone.1 | loop fusion | flops 3145728 | bytes 16777216 | tf_op jit(solution)/shard_map/while/body/eval_jaxpr/sub | solution.py:98
  145.7 2.0 %copy-done.2 = f32[1024,1024]{1,0:T(8,128)} copy-done((f32[1024,1024]{1,0:T(8,128)}, f32[1024,1024]{1,0:T(8,128)S(1)}, u32[]{:S(2)}) %copy-start.2) | copy-done | bytes 4194328 | tf_op jit(solution)/shard_map/while
  149.0 1.6 fusion.34
  151.0 1.8 copy-done.1
  152.8 2.7 %fusion.36 = f32[1024,1024]{1,0:T(8,128)S(1)} fusion(f32[128,8,8,128]{3,2,1,0:T(8,128)S(1)} %bitcast.62, f32[1024,1152]{1,0:T(8,128)S(1)} %fusion.34, f32[1024,1024]{1,0:T(8,128)S(1)} %copy-done.1, pred[]{:T(512)S(6)} %compare.14), kind=kLoop, calls=%fused_computation.3.clone.1 | loop fusion | flops 3145728 | bytes 16777216 | tf_op jit(solution)/shard_map/while/body/eval_jaxpr/sub | solution.py:98
  155.5 2.0 %copy-done.2 = f32[1024,1024]{1,0:T(8,128)} copy-done((f32[1024,1024]{1,0:T(8,128)}, f32[1024,1024]{1,0:T(8,128)S(1)}, u32[]{:S(2)}) %copy-start.2) | copy-done | bytes 4194328 | tf_op jit(solution)/shard_map/while
  158.8 1.6 fusion.34
  160.8 1.8 copy-done.1
  162.6 2.7 %fusion.36 = f32[1024,1024]{1,0:T(8,128)S(1)} fusion(f32[128,8,8,128]{3,2,1,0:T(8,128)S(1)} %bitcast.62, f32[1024,1152]{1,0:T(8,128)S(1)} %fusion.34, f32[1024,1024]{1,0:T(8,128)S(1)} %copy-done.1, pred[]{:T(512)S(6)} %compare.14), kind=kLoop, calls=%fused_computation.3.clone.1 | loop fusion | flops 3145728 | bytes 16777216 | tf_op jit(solution)/shard_map/while/body/eval_jaxpr/sub | solution.py:98
  165.3 2.0 %copy-done.2 = f32[1024,1024]{1,0:T(8,128)} copy-done((f32[1024,1024]{1,0:T(8,128)}, f32[1024,1024]{1,0:T(8,128)S(1)}, u32[]{:S(2)}) %copy-start.2) | copy-done | bytes 4194328 | tf_op jit(solution)/shard_map/while
  167.9 5.0 %multiply_bitcast_fusion = f32[1,1024,1024]{2,1,0:T(8,128)} fusion(f32[1024,1024]{1,0:T(8,128)} %get-tuple-element.97), kind=kLoop, calls=%fused_computation.18 | loop fusion | flops 1048576 | bytes 8388608 | tf_op jit(solution)/shard_map/broadcast_in_dim | solution.py:143
  (118 shorter events, 17.3 us)
Async XLA Ops:
  7.2 10.5 %copy-start = (bf16[2048,128]{1,0:T(8,128)(2,1)S(1)}, bf16[2048,128]{1,0:T(8,128)(2,1)}, u32[]{:S(2)}) copy-start(bf16[2048,128]{1,0:T(8,128)(2,1)} %param.6) | copy-start | bytes 1572868
  7.2 66.3 %copy-start.3 = (s32[2048]{0:T(1024)S(1)}, s32[2048]{0:T(1024)}, u32[]{:S(2)}) copy-start(s32[2048]{0:T(1024)} %param.9) | copy-start | bytes 24580
  7.2 65.4 %all-reduce.2.cloned.1.call-start = ((), (), s32[]{:S(2)}) async-start(), calls=%async_computation.1 | async-start | bytes 131072 | tf_op jit(solution)/shard_map/psum | solution.py:121
  22.2 57.2 %collective-permute-start = (bf16[1,8,128,128]{3,2,1,0:T(8,128)(2,1)S(1)}, bf16[1,8,128,128]{3,2,1,0:T(8,128)(2,1)S(1)}, u32[]{:S(2)}, u32[]{:S(2)}) collective-permute-start(bf16[1,8,128,128]{3,2,1,0:T(8,128)(2,1)S(1)} %constant_dynamic-slice_fusion.3), channel_id=1, source_target_pairs={{0,8},{8,16},{16,24},{24,0},{1,9},{9,17},{17,25},{25,1},{2,10},{10... | collective-permute-start | bytes 786440 | tf_op jit(solution)/shard_map/ppermute | solution.py:33
  75.8 9.1 %all-to-all-start = ((bf16[32,128,16]{1,2,0:T(8,128)(2,1)}), bf16[32,128,16]{1,2,0:T(8,128)(2,1)S(1)}, u32[]{:S(2)}, u32[]{:S(2)}) async-start(bf16[32,128,16]{1,2,0:T(8,128)(2,1)} %select_select_fusion.1), calls=%async_computation | async-start | bytes 262144 | tf_op jit(solution)/shard_map/all_to_all | solution.py:138
  79.6 9.4 %collective-permute-start.2 = (bf16[1,8,128,128]{3,2,1,0:T(8,128)(2,1)S(1)}, bf16[1,8,128,128]{3,2,1,0:T(8,128)(2,1)S(1)}, u32[]{:S(2)}, u32[]{:S(2)}) collective-permute-start(bf16[1,8,128,128]{3,2,1,0:T(8,128)(2,1)S(1)} %get-tuple-element.129), channel_id=1, source_target_pairs={{0,24},{8,0},{16,8},{24,16},{1,25},{9,1},{17,9},{25,17},{2,26},{10... | collective-permute-start | bytes 786440 | tf_op jit(solution)/shard_map/ppermute | solution.py:33
  82.5 6.4 %collective-permute-start.1 = (bf16[1,8,128,128]{3,2,1,0:T(8,128)(2,1)S(1)}, bf16[1,8,128,128]{3,2,1,0:T(8,128)(2,1)S(1)}, u32[]{:S(2)}, u32[]{:S(2)}) collective-permute-start(bf16[1,8,128,128]{3,2,1,0:T(8,128)(2,1)S(1)} %get-tuple-element.130), channel_id=1, source_target_pairs={{0,16},{8,24},{16,0},{24,8},{1,17},{9,25},{17,1},{25,9},{2,18},{10... | collective-permute-start | bytes 786440 | tf_op jit(solution)/shard_map/ppermute | solution.py:33
  91.9 2.2 %copy-start.1 = (f32[1024,1024]{1,0:T(8,128)S(1)}, f32[1024,1024]{1,0:T(8,128)}, u32[]{:S(2)}) copy-start(f32[1024,1024]{1,0:T(8,128)} %get-tuple-element.182) | copy-start | bytes 12582916 | tf_op jit(solution)/shard_map/while
  96.8 2.0 %copy-start.2 = (f32[1024,1024]{1,0:T(8,128)}, f32[1024,1024]{1,0:T(8,128)S(1)}, u32[]{:S(2)}) copy-start(f32[1024,1024]{1,0:T(8,128)S(1)} %fusion.36) | copy-start | bytes 12582916 | tf_op jit(solution)/shard_map/while
  101.7 2.2 %copy-start.1 = (f32[1024,1024]{1,0:T(8,128)S(1)}, f32[1024,1024]{1,0:T(8,128)}, u32[]{:S(2)}) copy-start(f32[1024,1024]{1,0:T(8,128)} %get-tuple-element.182) | copy-start | bytes 12582916 | tf_op jit(solution)/shard_map/while
  106.6 2.0 %copy-start.2 = (f32[1024,1024]{1,0:T(8,128)}, f32[1024,1024]{1,0:T(8,128)S(1)}, u32[]{:S(2)}) copy-start(f32[1024,1024]{1,0:T(8,128)S(1)} %fusion.36) | copy-start | bytes 12582916 | tf_op jit(solution)/shard_map/while
  111.5 2.2 %copy-start.1 = (f32[1024,1024]{1,0:T(8,128)S(1)}, f32[1024,1024]{1,0:T(8,128)}, u32[]{:S(2)}) copy-start(f32[1024,1024]{1,0:T(8,128)} %get-tuple-element.182) | copy-start | bytes 12582916 | tf_op jit(solution)/shard_map/while
  116.4 2.0 %copy-start.2 = (f32[1024,1024]{1,0:T(8,128)}, f32[1024,1024]{1,0:T(8,128)S(1)}, u32[]{:S(2)}) copy-start(f32[1024,1024]{1,0:T(8,128)S(1)} %fusion.36) | copy-start | bytes 12582916 | tf_op jit(solution)/shard_map/while
  121.3 2.2 %copy-start.1 = (f32[1024,1024]{1,0:T(8,128)S(1)}, f32[1024,1024]{1,0:T(8,128)}, u32[]{:S(2)}) copy-start(f32[1024,1024]{1,0:T(8,128)} %get-tuple-element.182) | copy-start | bytes 12582916 | tf_op jit(solution)/shard_map/while
  126.2 2.0 %copy-start.2 = (f32[1024,1024]{1,0:T(8,128)}, f32[1024,1024]{1,0:T(8,128)S(1)}, u32[]{:S(2)}) copy-start(f32[1024,1024]{1,0:T(8,128)S(1)} %fusion.36) | copy-start | bytes 12582916 | tf_op jit(solution)/shard_map/while
  131.0 2.2 %copy-start.1 = (f32[1024,1024]{1,0:T(8,128)S(1)}, f32[1024,1024]{1,0:T(8,128)}, u32[]{:S(2)}) copy-start(f32[1024,1024]{1,0:T(8,128)} %get-tuple-element.182) | copy-start | bytes 12582916 | tf_op jit(solution)/shard_map/while
  135.9 2.0 %copy-start.2 = (f32[1024,1024]{1,0:T(8,128)}, f32[1024,1024]{1,0:T(8,128)S(1)}, u32[]{:S(2)}) copy-start(f32[1024,1024]{1,0:T(8,128)S(1)} %fusion.36) | copy-start | bytes 12582916 | tf_op jit(solution)/shard_map/while
  140.8 2.2 %copy-start.1 = (f32[1024,1024]{1,0:T(8,128)S(1)}, f32[1024,1024]{1,0:T(8,128)}, u32[]{:S(2)}) copy-start(f32[1024,1024]{1,0:T(8,128)} %get-tuple-element.182) | copy-start | bytes 12582916 | tf_op jit(solution)/shard_map/while
  145.7 2.0 %copy-start.2 = (f32[1024,1024]{1,0:T(8,128)}, f32[1024,1024]{1,0:T(8,128)S(1)}, u32[]{:S(2)}) copy-start(f32[1024,1024]{1,0:T(8,128)S(1)} %fusion.36) | copy-start | bytes 12582916 | tf_op jit(solution)/shard_map/while
  150.6 2.2 %copy-start.1 = (f32[1024,1024]{1,0:T(8,128)S(1)}, f32[1024,1024]{1,0:T(8,128)}, u32[]{:S(2)}) copy-start(f32[1024,1024]{1,0:T(8,128)} %get-tuple-element.182) | copy-start | bytes 12582916 | tf_op jit(solution)/shard_map/while
  155.5 2.0 %copy-start.2 = (f32[1024,1024]{1,0:T(8,128)}, f32[1024,1024]{1,0:T(8,128)S(1)}, u32[]{:S(2)}) copy-start(f32[1024,1024]{1,0:T(8,128)S(1)} %fusion.36) | copy-start | bytes 12582916 | tf_op jit(solution)/shard_map/while
  160.4 2.2 %copy-start.1 = (f32[1024,1024]{1,0:T(8,128)S(1)}, f32[1024,1024]{1,0:T(8,128)}, u32[]{:S(2)}) copy-start(f32[1024,1024]{1,0:T(8,128)} %get-tuple-element.182) | copy-start | bytes 12582916 | tf_op jit(solution)/shard_map/while
  165.3 2.0 %copy-start.2 = (f32[1024,1024]{1,0:T(8,128)}, f32[1024,1024]{1,0:T(8,128)S(1)}, u32[]{:S(2)}) copy-start(f32[1024,1024]{1,0:T(8,128)S(1)} %fusion.36) | copy-start | bytes 12582916 | tf_op jit(solution)/shard_map/while
Sparse Core Ops, SparseCore 0:
  18.7 53.8 all-reduce.1
